TPU v7x, 256 devices: a whole 4x4x8 slice. The times are simulated.
256 devices in a mesh: sta: 16 (over y_lo, x, core), tm: 16 (over z, y_hi).
Axes of the slice: x: 4, y: 4 (y_hi: 2, y_lo: 2; y = y_hi * 2 + y_lo), z: 8, core: 2. Of those that a mesh axis runs over, the one named last changes fastest.
Arguments:
- waves: bfloat16 [3, 2048, 16, 512], P(None, 'sta', 'tm'), may hold values from -6 to 6
- partner: int32 [15, 16], replicated, may hold values from 0 to 15, as said below
- pair_count: int32 [16], P('sta'), may hold values from 192 to 256, as said below
- left_station: int32 [16, 256], P('sta'), may hold values from 0 to 127, as said below
- right_station: int32 [16, 256], P('sta'), may hold values from 0 to 127
- owner: int32 [16, 256], P('sta'), may hold values from 0 to 15, as said below
Outputs:
- stacks: float32 [8192, 2304], P('sta', 'tm')
Inputs may be any that keep to these rules, and one draw needn't show every extreme that they name: partner[k, i] = i XOR r_k, where r_0, ..., r_(14) are the numbers 1 to 15 in an order drawn from the seed. `pair_count`: each list's count is at least three quarters of 256; some list is full. Within one list the pairs (left_station, right_station) are all different. `owner`: among the first pair_count entries of a list, no block is named more than 32 times; one block, drawn from the seed, is named exactly 32 times in every list.
All inputs are finite; a program needn't handle non-finite values.
Results may differ from a plain program's by a relative error of at most 0.0032.
Values may be sent and summed in bfloat16 or wider, within the bound.
A program may use at most 64 MiB of HBM per device.

v0:
```python
import math

import jax
import jax.numpy as jnp
from jax import lax
from jax.sharding import PartitionSpec as P

LAGS = 256
HALF_BAND = 21


epsilon = 1e-06


def partner_2(value, axis, stride):
    mask = 2**stride
    pairs = [(source, source ^ mask) for source in range(lax.axis_size(axis))]
    return lax.ppermute(value, axis, pairs)


def make_dft_table(samples, freq_count):
    sample_index = jnp.arange(samples, dtype=jnp.int32)[:, None]
    freq_index = jnp.arange(freq_count, dtype=jnp.int32)[None, :]
    phases = (
        2.0 * math.pi / samples * jnp.mod(sample_index * freq_index, samples).astype(jnp.float32)
    )
    return jnp.concatenate([jnp.cos(phases), -jnp.sin(phases)], axis=1).astype(jnp.bfloat16)


def make_lag_table(samples, freq_count, lag_count):
    freq_index = jnp.arange(freq_count, dtype=jnp.int32)[:, None]
    lag_index = jnp.arange(lag_count, dtype=jnp.int32)[None, :] - lag_count // 2
    phases = 2.0 * math.pi / samples * jnp.mod(freq_index * lag_index, samples).astype(jnp.float32)
    return jnp.concatenate([jnp.cos(phases), -jnp.sin(phases)], axis=0)


def make_band(freq_count, half_band):
    freq_index = jnp.arange(freq_count, dtype=jnp.int32)
    band_matrix = (jnp.abs(freq_index[:, None] - freq_index[None, :]) <= half_band).astype(
        jnp.float32
    )
    return (band_matrix, jnp.sum(band_matrix, axis=0))


def whiten(records, dft_table, band_matrix, band_count):
    dims_in = records.shape
    spectra = jnp.dot(
        records.reshape(-1, dims_in[-1]), dft_table, preferred_element_type=jnp.float32
    )
    spectra = spectra.reshape(dims_in[:-1] + (dft_table.shape[1],))
    freq_count = dft_table.shape[1] // 2
    magnitude = jnp.sqrt(spectra[..., :freq_count] ** 2 + spectra[..., freq_count:] ** 2)
    amplitude = jnp.sum(magnitude, axis=-4)
    smooth = jnp.dot(
        amplitude.reshape(-1, freq_count), band_matrix, precision=lax.Precision.HIGHEST
    )
    smooth = smooth.reshape(amplitude.shape) / (3.0 * band_count) + epsilon
    smooth = jnp.concatenate([smooth, smooth], axis=-1)
    return spectra / jnp.expand_dims(smooth, -4)


def correlate(left_white, right_white, left_index, right_index, lag_table, scale):
    precise = lax.Precision.HIGHEST
    left_rows = jnp.take(left_white, left_index, axis=1)
    right_rows = jnp.take(right_white, right_index, axis=1)
    freq_count = left_rows.shape[-1] // 2
    left_real, left_imag = (left_rows[..., :freq_count], left_rows[..., freq_count:])
    right_real, right_imag = (right_rows[..., :freq_count], right_rows[..., freq_count:])
    cross_real = jnp.einsum(
        "apsf,bpsf->pabf", left_real, right_real, precision=precise
    ) + jnp.einsum("apsf,bpsf->pabf", left_imag, right_imag, precision=precise)
    cross_imag = jnp.einsum(
        "apsf,bpsf->pabf", left_imag, right_real, precision=precise
    ) - jnp.einsum("apsf,bpsf->pabf", left_real, right_imag, precision=precise)
    cross = jnp.concatenate([cross_real, cross_imag], axis=-1)
    lagged = jnp.einsum("pabg,gl->pabl", cross, lag_table, precision=precise) * scale
    return lagged.reshape(lagged.shape[0], -1)


def correlate_list(left_white, right_white, left_index, right_index, lag_table, scale):
    pair_total = left_index.shape[0]
    block_pairs = math.gcd(pair_total, 64)

    def one_block(indices):
        return correlate(left_white, right_white, indices[0], indices[1], lag_table, scale)

    lagged = lax.map(
        one_block, (left_index.reshape(-1, block_pairs), right_index.reshape(-1, block_pairs))
    )
    return lagged.reshape(pair_total, -1)


def slot_rows(owner_row, count, blocks, capacity):
    entry = jnp.arange(owner_row.shape[0], dtype=jnp.int32)
    valid = entry < count
    hits = (
        (owner_row[:, None] == jnp.arange(blocks, dtype=jnp.int32)[None, :]) & valid[:, None]
    ).astype(jnp.int32)
    before = jnp.cumsum(hits, axis=0) - hits
    rank = jnp.sum(before * hits, axis=1)
    return (jnp.where(valid, owner_row * capacity + rank, blocks * capacity), valid)


def local(waves, partner, pair_count, left_station, right_station, owner):
    sta_count = lax.axis_size("sta")
    tm_count = lax.axis_size("tm")
    seg_local = waves.shape[2]
    samples = waves.shape[3]
    freq_count = samples // 2
    pair_slots = left_station.shape[1]
    capacity = 2 * pair_slots // sta_count
    offset = partner[0, 0]
    partner_waves = waves
    for bit_index in range(sta_count.bit_length() - 1):
        taken = jnp.bitwise_and(jnp.right_shift(offset, bit_index), 1) == 1
        moved = partner_2(partner_waves, "sta", bit_index)
        partner_waves = jnp.where(taken, moved, partner_waves)
    dft_table = make_dft_table(samples, freq_count)
    band_matrix, band_count = make_band(freq_count, HALF_BAND)
    lag_table = make_lag_table(samples, freq_count, LAGS)
    white_both = whiten(jnp.stack([waves, partner_waves]), dft_table, band_matrix, band_count)
    scale = 1.0 / math.sqrt(freq_count * seg_local * tm_count)
    lagged = correlate_list(
        white_both[0], white_both[1], left_station[0], right_station[0], lag_table, scale
    )
    slot, valid = slot_rows(owner[0], pair_count[0], sta_count, capacity)
    partial_value = jnp.where(valid[:, None], lagged, jnp.zeros_like(lagged))
    outgoing = (
        jnp.zeros((sta_count * capacity, partial_value.shape[1]), jnp.float32)
        .at[slot]
        .add(partial_value, mode="drop")
    )
    received = lax.all_to_all(
        outgoing.reshape(sta_count, capacity, -1), "sta", split_axis=0, concat_axis=0, tiled=True
    )
    result = lax.psum_scatter(
        received.reshape(sta_count * capacity, -1), "tm", scatter_dimension=1, tiled=True
    )
    return result


def solution(mesh):
    in_specs = (
        P(None, "sta", "tm", None),
        P(),
        P("sta"),
        P("sta", None),
        P("sta", None),
        P("sta", None),
    )
    out_specs = P("sta", "tm")
    return jax.shard_map(local, mesh=mesh, in_specs=in_specs, out_specs=out_specs, check_vma=False)
```

profile of v0, /device:TPU:1, one launch (start us, length us, event | category | flops | bytes accessed | tf_op | source)
XLA Modules:
  0.0 370.7 jit_solution(13487382956941410020)
XLA Ops:
  6.5 3.2 collective-permute-start
  10.4 1.2 slice.35
  12.2 0.7 fusion.38
  12.9 1.1 broadcast_select_fusion
  13.9 0.1 collective-permute-start.1
  14.6 0.6 reduce-window.6
  15.3 0.2 slice_reduce_fusion
  15.4 9.2 %collective-permute-done.1 = bf16[3,128,1,512]{3,1,0,2:T(8,128)(2,1)S(1)} collective-permute-done((bf16[3,128,1,512]{3,1,0,2:T(8,128)(2,1)S(1)}, bf16[3,128,1,512]{3,1,0,2:T(8,128)(2,1)S(1)}, u32[]{:S(2)}, u32[]{:S(2)}) %collective-permute-start.1) | collective-permute-done | bytes 393248 | tf_op jit(solution)/shard_map/ppermute | solution.py:18
  24.7 1.1 collective-permute-start.2
  26.5 2.2 negate_convert_fusion
  28.7 1.0 fusion.31
  29.7 6.4 %collective-permute-done.2 = bf16[3,128,1,512]{3,1,0,2:T(8,128)(2,1)S(1)} collective-permute-done((bf16[3,128,1,512]{3,1,0,2:T(8,128)(2,1)S(1)}, bf16[3,128,1,512]{3,1,0,2:T(8,128)(2,1)S(1)}, u32[]{:S(2)}, u32[]{:S(2)}) %collective-permute-start.2) | collective-permute-done | bytes 393248 | tf_op jit(solution)/shard_map/ppermute | solution.py:18
  36.2 0.3 collective-permute-start.3
  37.1 0.5 broadcast.160
  37.7 0.6 reduce.10
  38.3 0.6 reduce.9
  39.2 6.2 %collective-permute-done.3 = bf16[3,128,1,512]{3,1,0,2:T(8,128)(2,1)S(1)} collective-permute-done((bf16[3,128,1,512]{3,1,0,2:T(8,128)(2,1)S(1)}, bf16[3,128,1,512]{3,1,0,2:T(8,128)(2,1)S(1)}, u32[]{:S(2)}, u32[]{:S(2)}) %collective-permute-start.3) | collective-permute-done | bytes 393248 | tf_op jit(solution)/shard_map/ppermute | solution.py:18
  45.5 0.6 fusion.17
  46.1 0.3 fusion.13
  46.4 0.3 fusion.10
  46.8 1.4 copy_divide_fusion
  48.1 1.3 slice_bitcast_fusion.4
  49.5 26.9 %while.10 = (s32[]{:T(128)}, f32[4,64,2304]{2,1,0:T(8,128)}, s32[4,64]{1,0:T(4,128)S(1)}, f32[3,128,1,512]{3,0,1,2:T(4,128)}, s32[4,64]{1,0:T(4,128)S(1)}, /*ind...) while((s32[]{:T(128)}, f32[4,64,2304]{2,1,0:T(8,128)}, s32[4,64]{1,0:T(4,128)S(1)}, ...), condition=%wide.region_6.8_spmd, body=%wide.region_5.7_spmd.sunk | while | flops 907496192 | bytes 14100837 | solution.py:87
  49.5 2.1 gather_fusion.1
  51.6 0.2 bitcast_select_fusion.6
  52.0 0.9 gather_fusion
  52.8 0.2 bitcast_select_fusion.5
  53.2 0.2 add_bitcast_fusion.4
  53.4 1.1 convolution_multiply_fusion.2
  54.5 0.4 copy.45
  54.9 0.4 broadcast_in_dim.76
  55.3 0.9 constant_dynamic-update-slice_fusion.2
  56.2 2.1 gather_fusion.1
  58.3 0.2 bitcast_select_fusion.6
  58.7 0.9 gather_fusion
  59.6 0.2 bitcast_select_fusion.5
  59.9 0.2 add_bitcast_fusion.4
  60.1 1.1 convolution_multiply_fusion.2
  61.2 0.4 copy.45
  61.6 0.4 broadcast_in_dim.76
  62.0 0.9 constant_dynamic-update-slice_fusion.2
  62.9 2.1 gather_fusion.1
  65.0 0.2 bitcast_select_fusion.6
  65.4 0.9 gather_fusion
  66.3 0.2 bitcast_select_fusion.5
  66.7 0.2 add_bitcast_fusion.4
  66.8 1.1 convolution_multiply_fusion.2
  67.9 0.4 copy.45
  68.3 0.4 broadcast_in_dim.76
  68.8 0.9 constant_dynamic-update-slice_fusion.2
  69.7 2.1 gather_fusion.1
  71.8 0.2 bitcast_select_fusion.6
  72.2 0.9 gather_fusion
  73.0 0.2 bitcast_select_fusion.5
  73.4 0.2 add_bitcast_fusion.4
  73.6 1.1 convolution_multiply_fusion.2
  74.7 0.4 copy.45
  75.1 0.4 broadcast_in_dim.76
  75.5 0.9 constant_dynamic-update-slice_fusion.2
  76.4 1.9 bitcast_select_fusion.2
  78.3 6.3 %scatter_custom_fusion = f32[512,2304]{1,0:T(8,128)} fusion(s32[256]{0:T(256)S(1)} %bitcast.135, f32[256,2304]{1,0:T(8,128)S(1)} %bitcast_select_fusion.2, f32[]{:T(128)} %constant.77.clone.1), kind=kCustom, calls=%fused_computation.29 | custom fusion | flops 589824 | bytes 4718596 | tf_op jit(solution)/shard_map/scatter-add | solution.py:131
  84.5 61.5 %all_to_all.5 = f32[16,32,2304]{2,1,0:T(8,128)} all-to-all(f32[16,32,2304]{2,1,0:T(8,128)} %bitcast.124), channel_id=1, replica_groups=mesh['sta'=16,'tm'=16] {'sta'}, dimensions={0} | all-to-all | bytes 9437184 | tf_op jit(solution)/shard_map/all_to_all | solution.py:133
  146.0 6.1 %copy.31 = f32[512,2304]{0,1:T(8,128)} copy(f32[512,2304]{1,0:T(8,128)} %bitcast.125) | data formatting | bytes 9437184
  152.2 211.7 %reduce-scatter.4.cloned.1.call-done = f32[144,512]{1,0:T(8,128)} async-done(((f32[2304,512]{1,0:T(8,128)}), f32[144,512]{1,0:T(8,128)}) %reduce-scatter.4.cloned.1.call-update) | async-done | bytes 294928
  (65 shorter events, 2.2 us)
Async XLA Ops:
  6.5 29.9 %copy-start.1 = (s32[1,256]{1,0:T(1,128)S(1)}, s32[1,256]{1,0:T(1,128)}, u32[]{:S(2)}) copy-start(s32[1,256]{1,0:T(1,128)} %param.15) | copy-start | bytes 3076
  6.5 357.4 %reduce-scatter.4.cloned.1.call-start = ((), (), s32[]{:S(2)}) async-start(), calls=%async_computation.2 | async-start | bytes 5013504
  6.5 6.3 %collective-permute-start = (bf16[3,128,1,512]{3,1,0,2:T(8,128)(2,1)}, bf16[3,128,1,512]{3,1,0,2:T(8,128)(2,1)S(1)}, u32[]{:S(2)}, u32[]{:S(2)}) collective-permute-start(bf16[3,128,1,512]{3,1,0,2:T(8,128)(2,1)} %bitcast.130), channel_id=1, source_target_pairs={{0,16},{16,0},{32,48},{48,32},{64,80},{80,64},{96,112},{112,96},{1... | collective-permute-start | bytes 1179656 | tf_op jit(solution)/shard_map/ppermute | solution.py:18
  12.2 25.5 %copy-start.2 = (s32[1,256]{1,0:T(1,128)S(1)}, s32[1,256]{1,0:T(1,128)}, u32[]{:S(2)}) copy-start(s32[1,256]{1,0:T(1,128)} %param.13) | copy-start | bytes 3076
  12.9 25.4 %copy-start.3 = (s32[1,256]{1,0:T(1,128)S(1)}, s32[1,256]{1,0:T(1,128)}, u32[]{:S(2)}) copy-start(s32[1,256]{1,0:T(1,128)} %param.14) | copy-start | bytes 3076
  13.9 10.8 %collective-permute-start.1 = (bf16[3,128,1,512]{3,1,0,2:T(8,128)(2,1)S(1)}, bf16[3,128,1,512]{3,1,0,2:T(8,128)(2,1)S(1)}, u32[]{:S(2)}, u32[]{:S(2)}) collective-permute-start(bf16[3,128,1,512]{3,1,0,2:T(8,128)(2,1)S(1)} %broadcast_select_fusion), channel_id=1, source_target_pairs={{0,32},{16,48},{32,0},{48,16},{64,96},{80,112},{96,64},{112,80},{1... | collective-permute-start | bytes 1179656 | tf_op jit(solution)/shard_map/ppermute | solution.py:18
  24.7 20.7 %copy-start = (bf16[3,128,1,512]{3,1,2,0:T(8,128)(2,1)S(1)}, bf16[3,128,1,512]{3,1,2,0:T(8,128)(2,1)}, u32[]{:S(2)}) copy-start(bf16[3,128,1,512]{3,1,2,0:T(8,128)(2,1)} %param.10) | copy-start | bytes 1179652
  24.7 11.4 %collective-permute-start.2 = (bf16[3,128,1,512]{3,1,0,2:T(8,128)(2,1)S(1)}, bf16[3,128,1,512]{3,1,0,2:T(8,128)(2,1)S(1)}, u32[]{:S(2)}, u32[]{:S(2)}) collective-permute-start(bf16[3,128,1,512]{3,1,0,2:T(8,128)(2,1)S(1)} %broadcast_select_fusion.1), channel_id=1, source_target_pairs={{0,64},{16,80},{32,96},{48,112},{64,0},{80,16},{96,32},{112,48},{1... | collective-permute-start | bytes 1179656 | tf_op jit(solution)/shard_map/ppermute | solution.py:18
  36.2 9.2 %collective-permute-start.3 = (bf16[3,128,1,512]{3,1,0,2:T(8,128)(2,1)S(1)}, bf16[3,128,1,512]{3,1,0,2:T(8,128)(2,1)S(1)}, u32[]{:S(2)}, u32[]{:S(2)}) collective-permute-start(bf16[3,128,1,512]{3,1,0,2:T(8,128)(2,1)S(1)} %broadcast_select_fusion.2), channel_id=1, source_target_pairs={{0,128},{16,144},{32,160},{48,176},{64,192},{80,208},{96,224},{112... | collective-permute-start | bytes 1179656 | tf_op jit(solution)/shard_map/ppermute | solution.py:18
Sparse Core Ops, SparseCore 0:
  152.3 211.5 reduce-scatter.3
where the time goes:
time: 375 us; the launch traced here: 371 us
  waiting for transfers between devices  234 us (62%)
  blocking collectives  61.5 us (16%)
  local copies, waits for them, and re-layouts  29.5 us (8%)
  other arithmetic  19.3 us (5%)
  between operations  16.5 us (4%)
  matrix products  5.21 us (1%)
  starting transfers between devices  4.69 us (1%)
    unnamed x2, waiting for transfers between devices  212 us
    all_to_all x1, blocking collectives, local(): lax.all_to_all(outgoing.reshape(sta_count, capacity, -1), 'sta', split_ax...  61.5 us
    ppermute x4, waiting for transfers between devices, partner_2(): return lax.ppermute(value, axis, pairs)  21.9 us
    gather x4, local copies, waits for them, and re-layouts, correlate(): right_rows = jnp.take(right_white, right_index, axis=1)  8.37 us
  transfers between devices with their start and end apart: 5, of which 4 were waited for; matrix products, arithmetic and copies ran while one was open for 2% of the time, Pallas kernels for 0%

commit v1 on v0

v1 whole, which is shorter than its diff:
```python
import functools
import math

import jax
import jax.numpy as jnp
import ml_dtypes
import numpy as np
from jax import lax
from jax.experimental import pallas as pl
from jax.experimental.pallas import tpu as pltpu
from jax.sharding import PartitionSpec as P

HALF_BAND = 21
SAMPLES = 512
FREQS = 256
LAGS = 256
EPSILON = 1e-6
BF16 = jnp.bfloat16
F32 = jnp.float32


def dft_table_t():
    f = np.arange(FREQS)[:, None]
    n = np.arange(SAMPLES)[None, :]
    angle = (2.0 * math.pi / SAMPLES) * np.mod(f * n, SAMPLES)
    table = np.concatenate([np.cos(angle), -np.sin(angle)], axis=0)
    return table.astype(np.float32).astype(ml_dtypes.bfloat16)


def lag_table(slices):
    f = np.arange(FREQS)[None, :]
    u = np.arange(LAGS)[:, None] - LAGS // 2
    angle = (2.0 * math.pi / SAMPLES) * np.mod(f * u, SAMPLES)
    scale = 1.0 / math.sqrt(FREQS * 16)
    width = FREQS // slices
    cos = (np.cos(angle) * scale).reshape(LAGS, slices, 1, width)
    sin = (-np.sin(angle) * scale).reshape(LAGS, slices, 1, width)
    table = np.concatenate([cos, sin], axis=2).reshape(LAGS, 2 * FREQS).astype(np.float32)
    high = table.astype(ml_dtypes.bfloat16)
    low = (table - high.astype(np.float32)).astype(ml_dtypes.bfloat16)
    return high, low


def dot(a, b):
    return jnp.dot(a, b, preferred_element_type=F32)


def dot_nt(a, b):
    return lax.dot_general(a, b, (((1,), (1,)), ((), ())), preferred_element_type=F32)


def halves(x):
    high = x.astype(BF16)
    return high, (x - high.astype(F32)).astype(BF16)


def whiten_kernel(waves_ref, table_ref, out_ref):
    slices, rows, stations = out_ref.shape
    width = FREQS // slices
    comps = waves_ref.shape[0] // stations
    spectra = dot_nt(table_ref[...], waves_ref[...])
    real, imag = spectra[:FREQS], spectra[FREQS:]
    magnitude = jnp.sqrt(real * real + imag * imag)
    amplitude = magnitude[:, :stations]
    for c in range(1, comps):
        amplitude = amplitude + magnitude[:, c * stations : (c + 1) * stations]
    row = lax.broadcasted_iota(jnp.int32, (FREQS, FREQS), 0)
    col = lax.broadcasted_iota(jnp.int32, (FREQS, FREQS), 1)
    band = (jnp.abs(row - col) <= HALF_BAND).astype(F32).astype(BF16)
    high, low = halves(amplitude)
    total = dot(band, high) + dot(band, low)
    f = lax.broadcasted_iota(jnp.int32, (FREQS, stations), 0)
    count = jnp.minimum(f + HALF_BAND, FREQS - 1) - jnp.maximum(f - HALF_BAND, 0) + 1
    smooth = total / (3.0 * count.astype(F32)) + EPSILON
    inverse = 1.0 / smooth
    for c in range(comps):
        lanes = slice(c * stations, (c + 1) * stations)
        for part, value in enumerate((real, imag)):
            white = (value[:, lanes] * inverse).astype(BF16)
            for s in range(slices):
                first = (c * 2 + part) * width
                out_ref[s, first : first + width, :] = white[s * width : (s + 1) * width]


def cross_kernel(comp_of, own_ref, other_ref, left_ref, right_ref, out_ref, left_rows, right_rows):
    segments, rows, stations = own_ref.shape
    pairs = left_ref.shape[1]
    width = rows // 6
    station = lax.broadcasted_iota(jnp.int32, (stations, pairs), 0)
    for ref, index_ref, gathered in (
        (own_ref, left_ref, left_rows),
        (other_ref, right_ref, right_rows),
    ):
        pick = (station == index_ref[...]).astype(F32).astype(BF16)
        gathered[...] = dot(ref[...].reshape(segments * rows, stations), pick)
    for lane in range(0, pairs, 128):
        for f0 in range(0, width, 8):

            def add(w, sums, lane=lane, f0=f0):
                base = w * rows + f0
                left = [left_rows[pl.ds(base + g * width, 8), lane : lane + 128] for g in range(6)]
                right = [right_rows[pl.ds(base + g * width, 8), lane : lane + 128] for g in range(6)]
                result = []
                for a in range(3):
                    for c in range(3):
                        lr, li = left[2 * a], left[2 * a + 1]
                        rr, ri = right[2 * c], right[2 * c + 1]
                        re, im = sums[2 * (3 * a + c)], sums[2 * (3 * a + c) + 1]
                        result += [re + (lr * rr + li * ri), im + (li * rr - lr * ri)]
                return tuple(result)

            zero = jnp.zeros((8, 128), F32)
            sums = lax.fori_loop(0, segments, add, (zero,) * 18, unroll=4)
            for s in range(len(comp_of)):
                for slot, comp in enumerate(comp_of[s]):
                    for part in range(2):
                        first = part * width + f0
                        out_ref[s, slot, first : first + 8, lane : lane + 128] = sums[
                            2 * comp + part
                        ].astype(out_ref.dtype)


def lag_kernel(capacity, cross_ref, high_ref, low_ref, edge_ref, owner_col, owner_row, count_ref, out_ref):
    slices, slots, rows, pairs = cross_ref.shape
    columns = high_ref.shape[0]
    parts = []
    for slot in range(slots):
        cross = cross_ref[:, slot].reshape(slices * rows, pairs)
        parts.append(dot(high_ref[...], cross) + dot(low_ref[...], cross))
    column = lax.broadcasted_iota(jnp.int32, (columns, pairs), 0)
    lagged = jnp.where(column < edge_ref[0], parts[0], parts[1])
    before = lax.broadcasted_iota(jnp.int32, (pairs, pairs), 0)
    entry = lax.broadcasted_iota(jnp.int32, (pairs, pairs), 1)
    same = (owner_col[...] == owner_row[...]) & (before < entry) & (before < count_ref[0])
    rank = jnp.sum(same.astype(F32), axis=0, keepdims=True).astype(jnp.int32)
    index = lax.broadcasted_iota(jnp.int32, (1, pairs), 1)
    target = jnp.where(index < count_ref[0], owner_row[...] * capacity + rank, -1)
    out_rows = out_ref.shape[0]
    place = lax.broadcasted_iota(jnp.int32, (out_rows, pairs), 0) == target
    place = place.astype(F32).astype(BF16)
    high, low = halves(lagged)
    out_ref[...] = dot_nt(place, high) + dot_nt(place, low)


VMEM = pl.BlockSpec(memory_space=pltpu.VMEM)
SMEM = pl.BlockSpec(memory_space=pltpu.SMEM)


def local(waves, partner, pair_count, left_station, right_station, owner):
    sta_count = lax.axis_size("sta")
    tm_count = lax.axis_size("tm")
    comps, stations, _, samples = waves.shape
    pairs = left_station.shape[1]
    capacity = 2 * pairs // sta_count
    width = FREQS // tm_count
    rows = 2 * comps * width
    columns = comps * comps * LAGS // tm_count
    comp_of = [(columns * s // LAGS, (columns * s + columns - 1) // LAGS) for s in range(tm_count)]

    white = pl.pallas_call(
        whiten_kernel,
        out_shape=jax.ShapeDtypeStruct((tm_count, rows, stations), BF16),
        in_specs=[VMEM, VMEM],
        out_specs=VMEM,
    )(waves.reshape(comps * stations, samples), jnp.asarray(dft_table_t()))
    own = lax.all_to_all(white, "tm", split_axis=0, concat_axis=0, tiled=True)

    def shift(offset, value):
        return lax.ppermute(value, "sta", [(i, i ^ offset) for i in range(sta_count)])

    other = lax.switch(
        partner[0, 0] - 1, [functools.partial(shift, r) for r in range(1, sta_count)], own
    )
    cross = pl.pallas_call(
        functools.partial(cross_kernel, comp_of),
        out_shape=jax.ShapeDtypeStruct((tm_count, 2, 2 * width, pairs), BF16),
        in_specs=[VMEM] * 4,
        out_specs=VMEM,
        scratch_shapes=[pltpu.VMEM((tm_count * rows, pairs), F32)] * 2,
    )(own, other, left_station, right_station)
    cross = lax.all_to_all(cross, "tm", split_axis=0, concat_axis=0, tiled=True)

    high, low = lag_table(tm_count)
    tm_index = lax.axis_index("tm")
    start = lax.rem(columns * tm_index, LAGS)
    edge = jnp.where(start + columns > LAGS, LAGS - start, columns).astype(jnp.int32)

    def column_rows(table):
        return lax.dynamic_slice_in_dim(
            jnp.asarray(np.concatenate([table, table[: columns]], axis=0)), start, columns, axis=0
        )

    outgoing = pl.pallas_call(
        functools.partial(lag_kernel, capacity),
        out_shape=jax.ShapeDtypeStruct((sta_count * capacity, columns), F32),
        in_specs=[VMEM, VMEM, VMEM, SMEM, VMEM, VMEM, SMEM],
        out_specs=VMEM,
    )(
        cross,
        column_rows(high),
        column_rows(low),
        edge.reshape(1),
        owner.reshape(pairs, 1),
        owner,
        pair_count,
    )
    received = lax.all_to_all(
        outgoing.reshape(sta_count, capacity, columns), "sta", split_axis=0, concat_axis=0, tiled=True
    )
    return received.reshape(sta_count * capacity, columns)


def solution(mesh):
    in_specs = (
        P(None, "sta", "tm", None),
        P(),
        P("sta"),
        P("sta", None),
        P("sta", None),
        P("sta", None),
    )
    return jax.shard_map(
        local, mesh=mesh, in_specs=in_specs, out_specs=P("sta", "tm"), check_vma=False
    )
```

time: 375 us -> 88.7 us (0.24)
  waiting for transfers between devices: 234 us -> 36.6 us
  blocking collectives: 61.5 us -> 15.7 us
  local copies, waits for them, and re-layouts: 29.5 us -> 6.07 us
  other arithmetic: 19.3 us -> 0 us
  between operations: 16.5 us -> 1.36 us
  starting transfers between devices: 4.69 us -> 19.7 us
  Pallas kernels: 0 us -> 8.52 us
  matrix products: 5.21 us -> 0 us
    unnamed x2 -> x0, waiting for transfers between devices: 212 us -> none
    all_to_all x1, blocking collectives: 61.5 us -> 15.7 us  [local(): lax.all_to_all(outgoing.reshape(sta_count, capacity, columns), 'sta', spl...]
    all_to_all x0 -> x2, waiting for transfers between devices: none -> 26.8 us  [the longest x1 13.7 us: local(): cross = lax.all_to_all(cross, 'tm', split_axis=0, concat_axis=0, tiled=True)]
    all_to_all x0 -> x2, starting transfers between devices: none -> 15.3 us  [the longest x1 11.7 us: local(): own = lax.all_to_all(white, 'tm', split_axis=0, concat_axis=0, tiled=True)]
    ppermute x4 -> x1, waiting for transfers between devices: 21.9 us -> 9.86 us  [shift(): lax.ppermute(value, 'sta', [(i, i ^ offset) for i in range(sta_count)])]
    gather x8 -> x0, local copies, waits for them, and re-layouts: 11.8 us -> none  [the longest x4 8.37 us: correlate(): right_rows = jnp.take(right_white, right_index, axis=1)]
    pallas_call x0 -> x3, Pallas kernels: none -> 8.52 us  [the longest x1 3.26 us: local(): pl.pallas_call(functools.partial(cross_kernel, comp_of), out_shape=jax.Sh...]
    scatter-add x1 -> x0, other arithmetic: 6.26 us -> none  [local(): outgoing = jnp.zeros((sta_count * capacity, partial_value.shape[1]), jnp....]
  transfers between devices with their start and end apart: 5 -> 3, of which waited for: 4 -> 3; matrix products, arithmetic and copies ran while one was open for 2% -> 4% of each run, Pallas kernels for 0% -> 0%
where the time goes in v1:
time: 88.7 us; the launch traced here: 87.9 us
  waiting for transfers between devices  36.6 us (41%)
  starting transfers between devices  19.7 us (22%)
  blocking collectives  15.7 us (18%)
  Pallas kernels  8.52 us (10%)
  local copies, waits for them, and re-layouts  6.07 us (7%)
  between operations  1.36 us (2%)
    all_to_all x1, blocking collectives, local(): lax.all_to_all(outgoing.reshape(sta_count, capacity, columns), 'sta', spl...  15.7 us
    all_to_all x1, waiting for transfers between devices, local(): cross = lax.all_to_all(cross, 'tm', split_axis=0, concat_axis=0, tiled=True)  13.7 us
    all_to_all x1, waiting for transfers between devices, local(): own = lax.all_to_all(white, 'tm', split_axis=0, concat_axis=0, tiled=True)  13 us
    all_to_all x1, starting transfers between devices, local(): own = lax.all_to_all(white, 'tm', split_axis=0, concat_axis=0, tiled=True)  11.7 us
    ppermute x1, waiting for transfers between devices, shift(): lax.ppermute(value, 'sta', [(i, i ^ offset) for i in range(sta_count)])  9.86 us
    ppermute x1, starting transfers between devices, shift(): lax.ppermute(value, 'sta', [(i, i ^ offset) for i in range(sta_count)])  4.36 us
    all_to_all x1, starting transfers between devices, local(): cross = lax.all_to_all(cross, 'tm', split_axis=0, concat_axis=0, tiled=True)  3.57 us
    pallas_call x1, Pallas kernels, local(): pl.pallas_call(functools.partial(cross_kernel, comp_of), out_shape=jax.Sh...  3.26 us
  transfers between devices with their start and end apart: 3, of which 3 were waited for; matrix products, arithmetic and copies ran while one was open for 4% of the time, Pallas kernels for 0%

profile of v1, /device:TPU:1, one launch (start us, length us, event | category | flops | bytes accessed | tf_op | source)
XLA Modules:
  0.0 87.9 jit_solution(8029333667650545061)
XLA Ops:
  0.0 2.7 %shard_map.91 = bf16[16,96,128]{2,1,0:T(8,128)(2,1)} custom-call(bf16[384,512]{1,0:T(8,128)(2,1)} %bitcast.8, bf16[512,512]{1,0:T(8,128)(2,1)} %constant.30.clone.table_ref), custom_call_target="tpu_custom_call" | custom-call | tf_op jit(solution)/shard_map/pallas_call | solution.py:160
  2.7 11.7 %all-to-all-start = ((bf16[16,96,128]{2,1,0:T(8,128)(2,1)}), bf16[16,96,128]{2,1,0:T(8,128)(2,1)S(1)}, u32[]{:S(2)}, u32[]{:S(2)}) async-start(bf16[16,96,128]{2,1,0:T(8,128)(2,1)} %shard_map.91), calls=%async_computation | async-start | bytes 786432 | tf_op jit(solution)/shard_map/all_to_all | solution.py:166
  14.4 1.2 %slice.3 = s32[1,1]{1,0:T(1,128)} slice(s32[15,16]{1,0:T(8,128)} %param.25), slice={[0:1], [0:1]} | slice | bytes 8 | tf_op jit(solution)/shard_map/slice | solution.py:172
  16.3 13.0 %all-to-all-done.own_ref = bf16[16,96,128]{2,1,0:T(8,128)(2,1)S(1)} async-done(((bf16[16,96,128]{2,1,0:T(8,128)(2,1)}), bf16[16,96,128]{2,1,0:T(8,128)(2,1)S(1)}, u32[]{:S(2)}, u32[]{:S(2)}) %all-to-all-start) | async-done | bytes 393248 | tf_op jit(solution)/shard_map/all_to_all | solution.py:166
  29.3 14.2 %conditional.1 = (bf16[16,96,128]{2,1,0:T(8,128)(2,1)}) conditional(s32[]{:T(128)} %bitcast.1, bf16[16,96,128]{2,1,0:T(8,128)(2,1)S(1)} %all-to-all-done.own_ref, bf16[16,96,128]{2,1,0:T(8,128)(2,1)S(1)} %all-to-all-done.own_ref, bf16[16,96,128]{2,1,0:T(8,128)(2,1)S(1)} %all-to-all-done.own_ref, ...), branch_computations={%region_0.0_spmd, %region_1.0_spmd, %region_2.0_spmd, %region_3.0_... | conditional | bytes 1572912 | solution.py:171
  29.3 4.4 %collective-permute-start.6 = (bf16[16,96,128]{2,1,0:T(8,128)(2,1)S(1)}, bf16[16,96,128]{2,1,0:T(8,128)(2,1)}, u32[]{:S(2)}, u32[]{:S(2)}) collective-permute-start(bf16[16,96,128]{2,1,0:T(8,128)(2,1)S(1)} %param.6), channel_id=1, source_target_pairs={{0,112},{16,96},{32,80},{48,64},{64,48},{80,32},{96,16},{112,0},{1... | collective-permute-start | bytes 1179656 | tf_op jit(solution)/shard_map/cond/branch_6_fun/ppermute | solution.py:169
  33.7 9.9 %collective-permute-done.6 = bf16[16,96,128]{2,1,0:T(8,128)(2,1)} collective-permute-done((bf16[16,96,128]{2,1,0:T(8,128)(2,1)S(1)}, bf16[16,96,128]{2,1,0:T(8,128)(2,1)}, u32[]{:S(2)}, u32[]{:S(2)}) %collective-permute-start.6) | collective-permute-done | bytes 393248 | tf_op jit(solution)/shard_map/cond/branch_6_fun/ppermute | solution.py:169
  43.5 3.3 %shard_map.92 = bf16[16,2,32,256]{3,2,1,0:T(8,128)(2,1)} custom-call(bf16[16,96,128]{2,1,0:T(8,128)(2,1)S(1)} %all-to-all-done.own_ref, bf16[16,96,128]{2,1,0:T(8,128)(2,1)} %get-tuple-element.38.other_ref, s32[1,256]{1,0:T(1,128)} %left_ref.1, s32[1,256]{1,0:T(1,128)} %right_ref.1), custom_call_target="tpu_custom_call" | custom-call | tf_op jit(solution)/shard_map/pallas_call | solution.py:174
  46.8 3.6 %all-to-all-start.1 = ((bf16[16,2,32,256]{3,2,1,0:T(8,128)(2,1)}), bf16[16,2,32,256]{3,2,1,0:T(8,128)(2,1)S(1)}, u32[]{:S(2)}, u32[]{:S(2)}) async-start(bf16[16,2,32,256]{3,2,1,0:T(8,128)(2,1)} %shard_map.92), calls=%async_computation.1 | async-start | bytes 1048576 | tf_op jit(solution)/shard_map/all_to_all | solution.py:181
  50.4 0.0 copy-start.1
  50.4 0.7 copy-done.1
  51.1 0.8 copy.11.owner_col
  52.5 1.7 %constant_dynamic-slice_fusion = (bf16[144,512]{1,0:T(8,128)(2,1)}, bf16[144,512]{1,0:T(8,128)(2,1)}) fusion(bf16[400,512]{1,0:T(8,128)(2,1)} %constant.32.clone, s32[]{:T(128)S(6)} %select_n.8, bf16[400,512]{1,0:T(8,128)(2,1)} %constant.31.clone), kind=kLoop, calls=%fused_computation | loop fusion | bytes 589828 | tf_op jit(solution)/shard_map/dynamic_slice | solution.py:189
  54.2 13.7 %all-to-all-done.1.cross_ref = bf16[16,2,32,256]{3,2,1,0:T(8,128)(2,1)S(1)} async-done(((bf16[16,2,32,256]{3,2,1,0:T(8,128)(2,1)}), bf16[16,2,32,256]{3,2,1,0:T(8,128)(2,1)S(1)}, u32[]{:S(2)}, u32[]{:S(2)}) %all-to-all-start.1) | async-done | bytes 524320 | tf_op jit(solution)/shard_map/all_to_all | solution.py:181
  68.0 0.0 copy-start
  68.0 0.8 copy-done
  68.8 2.6 %shard_map.93 = f32[512,144]{1,0:T(8,128)} custom-call(bf16[16,2,32,256]{3,2,1,0:T(8,128)(2,1)} %copy-done, bf16[144,512]{1,0:T(8,128)(2,1)} %get-tuple-element.37.high_ref, bf16[144,512]{1,0:T(8,128)(2,1)} %get-tuple-element.36.low_ref, s32[1]{0:T(128)} %bitcast.2.edge_ref, s32[256,1]{1,0:T(8,128)} %copy.11.owner_col, s32[1,256]{1,0:T(1,128)} %owner_row.1, ...), custom_call_target="tpu_custom_call" | custom-call | tf_op jit(solution)/shard_map/pallas_call | solution.py:193
  71.4 15.7 %all_to_all.60 = f32[16,32,144]{2,1,0:T(8,128)S(1)} all-to-all(f32[16,32,144]{2,1,0:T(8,128)} %bitcast.6), channel_id=1, replica_groups=mesh['sta'=16,'tm'=16] {'sta'}, dimensions={0} | all-to-all | bytes 589824 | tf_op jit(solution)/shard_map/all_to_all | solution.py:207
  87.1 0.9 %copy.12 = f32[512,144]{0,1:T(8,128)} copy(f32[512,144]{1,0:T(8,128)S(1)} %bitcast.7) | data formatting | bytes 589824 | tf_op jit(solution)/shard_map/reshape | solution.py:210
Async XLA Ops:
  2.7 26.6 %all-to-all-start = ((bf16[16,96,128]{2,1,0:T(8,128)(2,1)}), bf16[16,96,128]{2,1,0:T(8,128)(2,1)S(1)}, u32[]{:S(2)}, u32[]{:S(2)}) async-start(bf16[16,96,128]{2,1,0:T(8,128)(2,1)} %shard_map.91), calls=%async_computation | async-start | bytes 786432 | tf_op jit(solution)/shard_map/all_to_all | solution.py:166
  29.3 14.2 %collective-permute-start.6 = (bf16[16,96,128]{2,1,0:T(8,128)(2,1)S(1)}, bf16[16,96,128]{2,1,0:T(8,128)(2,1)}, u32[]{:S(2)}, u32[]{:S(2)}) collective-permute-start(bf16[16,96,128]{2,1,0:T(8,128)(2,1)S(1)} %param.6), channel_id=1, source_target_pairs={{0,112},{16,96},{32,80},{48,64},{64,48},{80,32},{96,16},{112,0},{1... | collective-permute-start | bytes 1179656 | tf_op jit(solution)/shard_map/cond/branch_6_fun/ppermute | solution.py:169
  46.8 21.2 %all-to-all-start.1 = ((bf16[16,2,32,256]{3,2,1,0:T(8,128)(2,1)}), bf16[16,2,32,256]{3,2,1,0:T(8,128)(2,1)S(1)}, u32[]{:S(2)}, u32[]{:S(2)}) async-start(bf16[16,2,32,256]{3,2,1,0:T(8,128)(2,1)} %shard_map.92), calls=%async_computation.1 | async-start | bytes 1048576 | tf_op jit(solution)/shard_map/all_to_all | solution.py:181
  50.4 0.7 copy-start.1
  68.0 0.8 copy-start

commit v2 on v1

--- a/solution.py
+++ b/solution.py
@@ -82,7 +82,80 @@
                 out_ref[s, first : first + width, :] = white[s * width : (s + 1) * width]
 
 
-def cross_kernel(comp_of, own_ref, other_ref, left_ref, right_ref, out_ref, left_rows, right_rows):
+def tm_peer(index, step, count):
+    high, low = index // 2, lax.rem(index, 2)
+    return lax.rem(high + step[0] + count // 2, count // 2) * 2 + lax.rem(low + step[1] + 2, 2)
+
+
+def tm_steps(count):
+    half = count // 2
+    steps = [(dz, dy) for dz in range(half) for dy in range(2) if (dz, dy) != (0, 0)]
+    return sorted(steps, key=lambda s: (-min(s[0], half - s[0]), -s[1], s[0]))
+
+
+def flip(index, offset):
+    bit = 1
+    while bit <= offset:
+        if offset & bit:
+            index = index + bit - 2 * bit * lax.rem(index // bit, 2)
+        bit *= 2
+    return index
+
+
+def spread_kernel(offset, white_ref, own_ref, other_ref, send, recv, pass_send, pass_recv):
+    count = white_ref.shape[0]
+    me, block = lax.axis_index("tm"), lax.axis_index("sta")
+    mate = {"sta": flip(block, offset), "tm": me}
+    steps = tm_steps(count)
+    barrier = pltpu.get_barrier_semaphore()
+
+    def peer(step):
+        return {"sta": block, "tm": tm_peer(me, step, count)}
+
+    def source(step):
+        return tm_peer(me, (-step[0], -step[1]), count)
+
+    for step in steps:
+        pl.semaphore_signal(barrier, inc=1, device_id=peer(step))
+    pl.semaphore_signal(barrier, inc=1, device_id=mate)
+    pl.semaphore_wait(barrier, len(steps) + 1)
+
+    def copy(k, step):
+        to = peer(step)
+        return pltpu.make_async_remote_copy(
+            white_ref.at[to["tm"]], own_ref.at[me], send.at[k], recv.at[k], device_id=to
+        )
+
+    def arrival(k, step):
+        at = source(step)
+        return pltpu.make_async_remote_copy(
+            white_ref.at[at], own_ref.at[at], send.at[k], recv.at[k], device_id=peer(step)
+        )
+
+    def onward(k, at, ref):
+        return pltpu.make_async_remote_copy(
+            ref.at[at], other_ref.at[at], pass_send.at[k], pass_recv.at[k], device_id=mate
+        )
+
+    last = len(steps)
+    sends = [copy(k, step) for k, step in enumerate(steps)]
+    for one in sends:
+        one.start()
+    passed = [onward(last, me, white_ref)]
+    passed[0].start()
+    own_ref[me] = white_ref[me]
+    for k, step in enumerate(steps):
+        arrival(k, step).wait_recv()
+        passed.append(onward(k, source(step), own_ref))
+        passed[-1].start()
+    for one in sends:
+        one.wait_send()
+    for one in passed:
+        one.wait_send()
+        one.wait_recv()
+
+
+def make_cross(comp_of, own_ref, other_ref, left_ref, right_ref, out_ref, left_rows, right_rows):
     segments, rows, stations = own_ref.shape
     pairs = left_ref.shape[1]
     width = rows // 6
@@ -120,7 +193,7 @@
                         ].astype(out_ref.dtype)
 
 
-def lag_kernel(capacity, cross_ref, high_ref, low_ref, edge_ref, owner_col, owner_row, count_ref, out_ref):
+def make_stacks(capacity, edge, cross_ref, high_ref, low_ref, owner_col, owner_row, count_ref, out_ref):
     slices, slots, rows, pairs = cross_ref.shape
     columns = high_ref.shape[0]
     parts = []
@@ -128,18 +201,108 @@
         cross = cross_ref[:, slot].reshape(slices * rows, pairs)
         parts.append(dot(high_ref[...], cross) + dot(low_ref[...], cross))
     column = lax.broadcasted_iota(jnp.int32, (columns, pairs), 0)
-    lagged = jnp.where(column < edge_ref[0], parts[0], parts[1])
+    lagged = jnp.where(column < edge, parts[0], parts[1])
     before = lax.broadcasted_iota(jnp.int32, (pairs, pairs), 0)
     entry = lax.broadcasted_iota(jnp.int32, (pairs, pairs), 1)
     same = (owner_col[...] == owner_row[...]) & (before < entry) & (before < count_ref[0])
     rank = jnp.sum(same.astype(F32), axis=0, keepdims=True).astype(jnp.int32)
     index = lax.broadcasted_iota(jnp.int32, (1, pairs), 1)
     target = jnp.where(index < count_ref[0], owner_row[...] * capacity + rank, -1)
-    out_rows = out_ref.shape[0]
-    place = lax.broadcasted_iota(jnp.int32, (out_rows, pairs), 0) == target
+    owners = out_ref.shape[0]
+    place = lax.broadcasted_iota(jnp.int32, (owners * capacity, pairs), 0) == target
     place = place.astype(F32).astype(BF16)
     high, low = halves(lagged)
-    out_ref[...] = dot_nt(place, high) + dot_nt(place, low)
+    stacks = dot_nt(place, high) + dot_nt(place, low)
+    out_ref[...] = stacks.reshape(owners, capacity, columns)
+
+
+def stack_kernel(
+    comp_of, capacity, own_ref, other_ref, left_ref, right_ref, high_ref, low_ref, owner_col,
+    owner_row, count_ref, out_ref, left_rows, right_rows, outgoing, cross, stacks,
+    send, recv, far_send, far_recv,
+):
+    count, slots = outgoing.shape[:2]
+    owners = stacks.shape[0]
+    columns = high_ref.shape[0]
+    me, block = lax.axis_index("tm"), lax.axis_index("sta")
+    steps = tm_steps(count)
+    barrier = pltpu.get_barrier_semaphore()
+
+    def peer(step):
+        return {"sta": block, "tm": tm_peer(me, step, count)}
+
+    def source(step):
+        return tm_peer(me, (-step[0], -step[1]), count)
+
+    def start_of(index):
+        return lax.rem(columns * index, LAGS)
+
+    def double(index):
+        return start_of(index) + columns > LAGS
+
+    def far(step):
+        return {"sta": lax.rem(block + step + owners, owners), "tm": me}
+
+    for step in steps:
+        pl.semaphore_signal(barrier, inc=1, device_id=peer(step))
+    for step in range(1, owners):
+        pl.semaphore_signal(barrier, inc=1, device_id=far(step))
+    make_cross(comp_of, own_ref, other_ref, left_ref, right_ref, outgoing, left_rows, right_rows)
+    pl.semaphore_wait(barrier, len(steps) + owners - 1)
+
+    def copy(k, slot, at, to, step):
+        return pltpu.make_async_remote_copy(
+            outgoing.at[at, slot], cross.at[to, slot], send.at[k, slot], recv.at[k, slot],
+            device_id=peer(step),
+        )
+
+    for k, step in enumerate(steps):
+        at = peer(step)["tm"]
+        copy(k, 0, at, me, step).start()
+
+        @pl.when(double(at))
+        def _():
+            copy(k, 1, at, me, step).start()
+
+    cross[me] = outgoing[me]
+
+    @pl.when(jnp.logical_not(double(me)))
+    def _():
+        for s in range(count):
+            cross[s, 1] = jnp.zeros(cross.shape[2:], cross.dtype)
+
+    for k, step in enumerate(steps):
+        at = source(step)
+        copy(k, 0, at, at, step).wait_recv()
+
+        @pl.when(double(me))
+        def _():
+            copy(k, 1, at, at, step).wait_recv()
+
+    edge = LAGS - start_of(me)
+    make_stacks(capacity, edge, cross, high_ref, low_ref, owner_col, owner_row, count_ref, stacks)
+
+    def away(k, at, to, step):
+        return pltpu.make_async_remote_copy(
+            stacks.at[at], out_ref.at[to], far_send.at[k], far_recv.at[k], device_id=far(step)
+        )
+
+    for step in range(1, owners):
+        away(step, far(step)["sta"], block, step).start()
+    out_ref[block] = stacks[block]
+    for k, step in enumerate(steps):
+        at = peer(step)["tm"]
+        copy(k, 0, at, me, step).wait_send()
+
+        @pl.when(double(at))
+        def _():
+            copy(k, 1, at, me, step).wait_send()
+
+    for step in range(1, owners):
+        at = far(-step)["sta"]
+        away(step, at, at, step).wait_recv()
+    for step in range(1, owners):
+        away(step, far(step)["sta"], block, step).wait_send()
 
 
 VMEM = pl.BlockSpec(memory_space=pltpu.VMEM)
@@ -163,51 +326,58 @@
         in_specs=[VMEM, VMEM],
         out_specs=VMEM,
     )(waves.reshape(comps * stations, samples), jnp.asarray(dft_table_t()))
-    own = lax.all_to_all(white, "tm", split_axis=0, concat_axis=0, tiled=True)
-
-    def shift(offset, value):
-        return lax.ppermute(value, "sta", [(i, i ^ offset) for i in range(sta_count)])
-
-    other = lax.switch(
-        partner[0, 0] - 1, [functools.partial(shift, r) for r in range(1, sta_count)], own
+
+    def exchange(offset, value):
+        return pl.pallas_call(
+            functools.partial(spread_kernel, offset),
+            out_shape=[jax.ShapeDtypeStruct(value.shape, value.dtype)] * 2,
+            in_specs=[VMEM],
+            out_specs=[VMEM, VMEM],
+            scratch_shapes=[pltpu.SemaphoreType.DMA((tm_count,))] * 4,
+            compiler_params=pltpu.CompilerParams(collective_id=offset, has_side_effects=True),
+        )(value)
+
+    own, other = lax.switch(
+        partner[0, 0] - 1, [functools.partial(exchange, r) for r in range(1, sta_count)], white
     )
-    cross = pl.pallas_call(
-        functools.partial(cross_kernel, comp_of),
-        out_shape=jax.ShapeDtypeStruct((tm_count, 2, 2 * width, pairs), BF16),
-        in_specs=[VMEM] * 4,
-        out_specs=VMEM,
-        scratch_shapes=[pltpu.VMEM((tm_count * rows, pairs), F32)] * 2,
-    )(own, other, left_station, right_station)
-    cross = lax.all_to_all(cross, "tm", split_axis=0, concat_axis=0, tiled=True)
 
     high, low = lag_table(tm_count)
     tm_index = lax.axis_index("tm")
     start = lax.rem(columns * tm_index, LAGS)
-    edge = jnp.where(start + columns > LAGS, LAGS - start, columns).astype(jnp.int32)
-
     def column_rows(table):
         return lax.dynamic_slice_in_dim(
             jnp.asarray(np.concatenate([table, table[: columns]], axis=0)), start, columns, axis=0
         )
 
-    outgoing = pl.pallas_call(
-        functools.partial(lag_kernel, capacity),
-        out_shape=jax.ShapeDtypeStruct((sta_count * capacity, columns), F32),
-        in_specs=[VMEM, VMEM, VMEM, SMEM, VMEM, VMEM, SMEM],
+    result = pl.pallas_call(
+        functools.partial(stack_kernel, comp_of, capacity),
+        out_shape=jax.ShapeDtypeStruct((sta_count, capacity, columns), F32),
+        in_specs=[VMEM] * 8 + [SMEM],
         out_specs=VMEM,
+        scratch_shapes=[
+            pltpu.VMEM((tm_count * rows, pairs), F32),
+            pltpu.VMEM((tm_count * rows, pairs), F32),
+            pltpu.VMEM((tm_count, 2, 2 * width, pairs), BF16),
+            pltpu.VMEM((tm_count, 2, 2 * width, pairs), BF16),
+            pltpu.VMEM((sta_count, capacity, columns), F32),
+            pltpu.SemaphoreType.DMA((tm_count, 2)),
+            pltpu.SemaphoreType.DMA((tm_count, 2)),
+            pltpu.SemaphoreType.DMA((sta_count,)),
+            pltpu.SemaphoreType.DMA((sta_count,)),
+        ],
+        compiler_params=pltpu.CompilerParams(collective_id=0, has_side_effects=True),
     )(
-        cross,
+        own,
+        other,
+        left_station,
+        right_station,
         column_rows(high),
         column_rows(low),
-        edge.reshape(1),
         owner.reshape(pairs, 1),
         owner,
         pair_count,
     )
-    received = lax.all_to_all(
-        outgoing.reshape(sta_count, capacity, columns), "sta", split_axis=0, concat_axis=0, tiled=True
-    )
-    return received.reshape(sta_count * capacity, columns)
+    return result.reshape(sta_count * capacity, columns)
 
 
 def solution(mesh):

time: 88.7 us -> 65.2 us (0.74)
  Pallas kernels: 8.52 us -> 57 us
  waiting for transfers between devices: 36.6 us -> 0 us
  starting transfers between devices: 19.7 us -> 0 us
  blocking collectives: 15.7 us -> 0 us
    pallas_call x2, Pallas kernels: 5.86 us -> 55.1 us  [the longest x1 27.9 us: exchange(): pl.pallas_call(functools.partial(spread_kernel, offset), out_shape=[jax.S...]
    all_to_all x2 -> x0, waiting for transfers between devices: 26.8 us -> none  [the longest x1 13.7 us: local(): cross = lax.all_to_all(cross, 'tm', split_axis=0, concat_axis=0, tiled=True)]
    all_to_all x1 -> x0, blocking collectives: 15.7 us -> none  [local(): lax.all_to_all(outgoing.reshape(sta_count, capacity, columns), 'sta', spl...]
    all_to_all x2 -> x0, starting transfers between devices: 15.3 us -> none  [the longest x1 11.7 us: local(): own = lax.all_to_all(white, 'tm', split_axis=0, concat_axis=0, tiled=True)]
    ppermute x1 -> x0, waiting for transfers between devices: 9.86 us -> none  [shift(): lax.ppermute(value, 'sta', [(i, i ^ offset) for i in range(sta_count)])]
    ppermute x1 -> x0, starting transfers between devices: 4.36 us -> none  [shift(): lax.ppermute(value, 'sta', [(i, i ^ offset) for i in range(sta_count)])]
    reshape x1, local copies, waits for them, and re-layouts: 0.89 us -> 1.93 us  [local(): return result.reshape(sta_count * capacity, columns)]
  transfers between devices with their start and end apart: 3 -> 0, of which waited for: 3 -> 0; matrix products, arithmetic and copies ran while one was open for 4% -> 0% of each run, Pallas kernels for 0% -> 0%
where the time goes in v2:
time: 65.2 us; the launch traced here: 64.9 us
  Pallas kernels  57 us (87%)
  local copies, waits for them, and re-layouts  6.31 us (10%)
  between operations  1.34 us (2%)
    pallas_call x1, Pallas kernels, exchange(): pl.pallas_call(functools.partial(spread_kernel, offset), out_shape=[jax.S...  27.9 us
    pallas_call x1, Pallas kernels, local(): pl.pallas_call(functools.partial(stack_kernel, comp_of, capacity), out_sh...  27.2 us
    reshape x1, local copies, waits for them, and re-layouts, local(): return result.reshape(sta_count * capacity, columns)  1.93 us
    pallas_call x1, Pallas kernels, local(): pl.pallas_call(whiten_kernel, out_shape=jax.ShapeDtypeStruct((tm_count, r...  1.91 us
    dynamic_slice x1, local copies, waits for them, and re-layouts, column_rows(): lax.dynamic_slice_in_dim(jnp.asarray(np.concatenate([table, table[:column...  1.71 us

profile of v2, /device:TPU:1, one launch (start us, length us, event | category | flops | bytes accessed | tf_op | source)
XLA Modules:
  0.0 64.9 jit_solution(14636815782546131586)
XLA Ops:
  0.0 1.2 %slice.3 = s32[1,1]{1,0:T(1,128)} slice(s32[15,16]{1,0:T(8,128)} %param.25), slice={[0:1], [0:1]} | slice | bytes 8 | tf_op jit(solution)/shard_map/slice | solution.py:341
  1.9 1.9 %shard_map.91 = bf16[16,96,128]{2,1,0:T(8,128)(2,1)S(1)} custom-call(bf16[384,512]{1,0:T(8,128)(2,1)} %bitcast.5, bf16[512,512]{1,0:T(8,128)(2,1)} %constant.29.clone.table_ref), custom_call_target="tpu_custom_call" | custom-call | tf_op jit(solution)/shard_map/pallas_call | solution.py:323
  3.8 28.1 %conditional.1 = ((bf16[16,96,128]{2,1,0:T(8,128)(2,1)S(1)}, bf16[16,96,128]{2,1,0:T(8,128)(2,1)S(1)})) conditional(s32[]{:T(128)} %bitcast, bf16[16,96,128]{2,1,0:T(8,128)(2,1)S(1)} %shard_map.91, bf16[16,96,128]{2,1,0:T(8,128)(2,1)S(1)} %shard_map.91, bf16[16,96,128]{2,1,0:T(8,128)(2,1)S(1)} %shard_map.91, ...), branch_computations={%region_0.0_spmd, %region_1.0_spmd, %region_2.0_spmd, %region_3.0_... | conditional | bytes 8 | solution.py:340
  3.8 27.9 %branch_6_fun.1 = (bf16[16,96,128]{2,1,0:T(8,128)(2,1)S(1)}, bf16[16,96,128]{2,1,0:T(8,128)(2,1)S(1)}) custom-call(bf16[16,96,128]{2,1,0:T(8,128)(2,1)S(1)} %white_ref.6), custom_call_target="tpu_custom_call" | custom-call | tf_op jit(solution)/shard_map/cond/branch_6_fun/pallas_call | solution.py:331
  31.9 1.7 %constant_dynamic-slice_fusion = (bf16[144,512]{1,0:T(8,128)(2,1)}, bf16[144,512]{1,0:T(8,128)(2,1)}) fusion(bf16[400,512]{1,0:T(8,128)(2,1)} %constant.31.clone, s32[]{:T(128)S(6)} %select_n.4, bf16[400,512]{1,0:T(8,128)(2,1)} %constant.30.clone), kind=kLoop, calls=%fused_computation | loop fusion | bytes 589828 | tf_op jit(solution)/shard_map/dynamic_slice | solution.py:348
  33.6 0.0 copy-start
  33.6 0.7 %copy-done = s32[1,256]{1,0:T(1,128)S(1)} copy-done((s32[1,256]{1,0:T(1,128)S(1)}, s32[1,256]{1,0:T(1,128)}, u32[]{:S(2)}) %copy-start) | copy-done | bytes 1048
  34.3 0.8 %copy.11.owner_col = s32[256,1]{1,0:T(8,128)} copy(s32[256,1]{0,1:T(1,128)S(1)} %bitcast.6) | data formatting | bytes 2048 | tf_op jit(solution)/shard_map/reshape | solution.py:376
  35.8 27.2 %shard_map.92 = f32[16,32,144]{2,1,0:T(8,128)} custom-call(bf16[16,96,128]{2,1,0:T(8,128)(2,1)S(1)} %get-tuple-element.22.own_ref, bf16[16,96,128]{2,1,0:T(8,128)(2,1)S(1)} %get-tuple-element.23.other_ref, s32[1,256]{1,0:T(1,128)} %left_ref.1, s32[1,256]{1,0:T(1,128)} %right_ref.1, bf16[144,512]{1,0:T(8,128)(2,1)} %get-tuple-element.25.high_ref, ...), custom_call_target="tpu_custom_call" | custom-call | tf_op jit(solution)/shard_map/pallas_call | solution.py:352
  63.0 1.9 %copy.12 = f32[512,144]{0,1:T(8,128)} copy(f32[512,144]{1,0:T(8,128)} %bitcast.4) | data formatting | bytes 589824 | tf_op jit(solution)/shard_map/reshape | solution.py:380
Async XLA Ops:
  33.6 0.7 %copy-start = (s32[1,256]{1,0:T(1,128)S(1)}, s32[1,256]{1,0:T(1,128)}, u32[]{:S(2)}) copy-start(s32[1,256]{1,0:T(1,128)} %owner_row.1) | copy-start | bytes 3076
